TPU v7x, 32 devices: a whole 2x2x4 slice. The times are simulated.
32 devices in a mesh: grp: 4 (over z), pen: 8 (over y, x, core).
Axes of the slice: x: 2, y: 2, z: 4, core: 2. Of those that a mesh axis runs over, the one named last changes fastest.
Arguments:
- cell_offsets: int32 [2, 1048576], P(None, ('grp', 'pen')), may hold values from 0 to 1
- cell_z: int32 [1048576], P(('grp', 'pen')), may hold values from 0 to 255
- frac: float32 [3, 1048576], P(None, ('grp', 'pen')), may hold values from 0 to 1
- charges: float32 [1048576], P(('grp', 'pen')), may hold values from -4 to 4
- tile_counts: int32 [16384], P(('grp', 'pen')), may hold values from 16 to 64, as said below
Outputs:
- forces: float32 [3, 1048576], P(None, ('grp', 'pen'))
- energy: float32 [], replicated
Inputs may be any that keep to these rules, and one draw needn't show every extreme that they name: `tile_counts`: live slots of each tile; some tile holds 64.
All inputs are finite; a program needn't handle non-finite values.
Results may differ from a plain program's by a relative error of at most 0.0003.
Values sent between devices are 32-bit elements; how exact they have to be, the bound alone decides.
A program may use at most 256 MiB of HBM per device.

v0:
```python
import math
import jax
import jax.numpy as jnp
from jax import lax
from jax.sharding import PartitionSpec as P

KX = 256
KY = 256
KZ = 256
ATOMS = 1048576
ewald_split = 0.6
highest = lax.Precision.HIGHEST


def shifted(block, axis, distance):
    devices = range(lax.axis_size(axis))
    route = [((i - distance) % len(devices), i) for i in devices]
    return lax.ppermute(block, axis, route)


def spline_rows(fracs):
    values = [jnp.ones_like(fracs)]
    fifth = values
    for order in range(2, 7):
        nxt = []
        for j in range(order):
            term = jnp.zeros_like(fracs)
            if j >= 1:
                term = values[j - 1] * (fracs + order - 1 - j)
            if j <= order - 2:
                term = term + values[j] * (1.0 - fracs + j)
            nxt.append(term / (order - 1))
        if order == 5:
            fifth = nxt
        values = nxt
    slopes = []
    for j in range(6):
        term = jnp.zeros_like(fracs)
        if j >= 1:
            term = fifth[j - 1]
        if j <= 4:
            term = term - fifth[j]
        slopes.append(term)
    return (values, slopes)


def tile_weights(offsets, zcell, fracs, charge, counts, size_z):
    slots = charge.shape[-1]
    live = (jnp.arange(slots, dtype=jnp.int32) < counts[..., None]).astype(jnp.float32)
    live_q = charge * live
    theta_x, slope_x = spline_rows(fracs[0])
    theta_y, slope_y = spline_rows(fracs[1])
    theta_z, slope_z = spline_rows(fracs[2])
    footing = jnp.arange(8, dtype=jnp.int32)[:, None]
    cells = jnp.arange(size_z, dtype=jnp.int32)
    weight_x = 0.0
    grade_x = 0.0
    weight_y = 0.0
    grade_y = 0.0
    weight_z = 0.0
    grade_z = 0.0
    for j in range(6):
        hit_x = (footing == offsets[0][..., None, :] + j).astype(jnp.float32)
        hit_y = (footing == offsets[1][..., None, :] + j).astype(jnp.float32)
        hit_z = (cells == (zcell[..., :, None] + j) % size_z).astype(jnp.float32)
        weight_x = weight_x + theta_x[j][..., None, :] * hit_x
        grade_x = grade_x + slope_x[j][..., None, :] * hit_x
        weight_y = weight_y + theta_y[j][..., None, :] * hit_y
        grade_y = grade_y + slope_y[j][..., None, :] * hit_y
        weight_z = weight_z + theta_z[j][..., :, None] * hit_z
        grade_z = grade_z + slope_z[j][..., :, None] * hit_z
    return (weight_x, grade_x, weight_y, grade_y, weight_z, grade_z, live_q)


def modulus(index, length):
    coeffs = (1.0 / 120.0, 26.0 / 120.0, 66.0 / 120.0, 26.0 / 120.0, 1.0 / 120.0)
    real_part = 0.0
    imag_part = 0.0
    for j in range(5):
        angle = (index * j % length).astype(jnp.float32) * (2.0 * math.pi / length)
        real_part = real_part + coeffs[j] * jnp.cos(angle)
        imag_part = imag_part + coeffs[j] * jnp.sin(angle)
    return real_part * real_part + imag_part * imag_part


def influence(index_x, index_y, index_z):
    freq_x = jnp.where(2 * index_x < KX, index_x, index_x - KX).astype(jnp.float32) / KX
    freq_y = jnp.where(2 * index_y < KY, index_y, index_y - KY).astype(jnp.float32) / KY
    freq_z = jnp.where(2 * index_z < KZ, index_z, index_z - KZ).astype(jnp.float32) / KZ
    square = freq_x * freq_x + freq_y * freq_y + freq_z * freq_z
    safe = jnp.where(square > 0, square, 1.0)
    volume = float(KX * KY * KZ)
    value = jnp.exp(-math.pi**2 * safe / ewald_split**2) / (math.pi * volume * safe)
    value = value / (modulus(index_x, KX) * modulus(index_y, KY) * modulus(index_z, KZ))
    return jnp.where(square > 0, value, 0.0)


def dft_tables(length):
    index = jnp.arange(length, dtype=jnp.int32)
    angle = (index[:, None] * index[None, :] % length).astype(jnp.float32) * (
        2.0 * math.pi / length
    )
    return (jnp.cos(angle), jnp.sin(angle))


def z_slots(groups):
    planes = KZ // (2 * groups) + 1
    owner = jnp.arange(groups, dtype=jnp.int32)[:, None]
    within = jnp.arange(planes, dtype=jnp.int32)[None, :]
    ordinary = owner * (planes - 1) + within
    frequency = jnp.where(within < planes - 1, ordinary, jnp.where(owner == 0, KZ // 2, 0))
    plane_weight = jnp.where(
        within < planes - 1, jnp.where(frequency == 0, 1.0, 2.0), jnp.where(owner == 0, 1.0, 0.0)
    )
    frequency = frequency.reshape(-1)
    plane_weight = plane_weight.reshape(-1).astype(jnp.float32)
    position = jnp.arange(KZ, dtype=jnp.int32)
    angle = (frequency[:, None] * position[None, :] % KZ).astype(jnp.float32) * (2.0 * math.pi / KZ)
    usable = (plane_weight > 0).astype(jnp.float32)[:, None]
    return (planes, frequency, plane_weight, jnp.cos(angle) * usable, jnp.sin(angle) * usable)


def forward_complex(data, cos_table, sin_table, shape, axis):
    direct = jnp.dot(cos_table, data, precision=highest).reshape(shape)
    other = jnp.dot(sin_table, data, precision=highest).reshape(shape)
    real_part = jnp.take(direct, 0, axis=axis) + jnp.take(other, 1, axis=axis)
    imag_part = jnp.take(direct, 1, axis=axis) - jnp.take(other, 0, axis=axis)
    return (real_part, imag_part)


def inverse_complex(data, cos_table, sin_table, shape, axis):
    direct = jnp.dot(cos_table, data, precision=highest).reshape(shape)
    other = jnp.dot(sin_table, data, precision=highest).reshape(shape)
    real_part = jnp.take(direct, 0, axis=axis) - jnp.take(other, 1, axis=axis)
    imag_part = jnp.take(other, 0, axis=axis) + jnp.take(direct, 1, axis=axis)
    return (real_part, imag_part)


def spectrum_pen_first(grid, block_x, block_y):
    cos_x, sin_x = dft_tables(KX)
    cos_y, sin_y = dft_tables(KY)
    planes, frequency, plane_weight, cos_z, sin_z = z_slots(lax.axis_size("pen"))
    slot_total = cos_z.shape[0]
    lines = KY // lax.axis_size("grp")
    real_z = jnp.einsum("xyz,kz->ykx", grid, cos_z, precision=highest)
    imag_z = -jnp.einsum("xyz,kz->ykx", grid, sin_z, precision=highest)
    outgoing = jnp.stack([real_z, imag_z], axis=2).reshape(block_y, slot_total * 2 * block_x)
    columns = lax.all_to_all(outgoing, "pen", split_axis=1, concat_axis=0, tiled=True)
    real_y, imag_y = forward_complex(columns, cos_y, sin_y, (KY, planes, 2, block_x), 2)
    sectioned = jnp.transpose(jnp.stack([real_y, imag_y], axis=-1), (2, 0, 1, 3)).reshape(
        block_x, KY * planes * 2
    )
    rows = lax.all_to_all(sectioned, "grp", split_axis=1, concat_axis=0, tiled=True)
    real_x, imag_x = forward_complex(rows, cos_x, sin_x, (KX, lines, planes, 2), 3)
    first = lax.axis_index("pen") * planes
    index_x = jnp.arange(KX, dtype=jnp.int32)[:, None, None]
    index_y = lax.axis_index("grp") * lines + jnp.arange(lines, dtype=jnp.int32)[None, :, None]
    index_z = lax.dynamic_slice_in_dim(frequency, first, planes)[None, None, :]
    local_weight = lax.dynamic_slice_in_dim(plane_weight, first, planes)[None, None, :]
    kernel = influence(index_x, index_y, index_z)
    spectral = 0.5 * jnp.sum(local_weight * kernel * (real_x * real_x + imag_x * imag_x))
    scaled = jnp.stack([kernel * real_x, kernel * imag_x], axis=-1).reshape(KX, lines * planes * 2)
    real_b, imag_b = inverse_complex(scaled, cos_x, sin_x, (KX, lines, planes, 2), 3)
    returning = jnp.stack([real_b, imag_b], axis=-1).reshape(KX, lines * planes * 2)
    rows_home = lax.all_to_all(returning, "grp", split_axis=0, concat_axis=1, tiled=True)
    rows_home = jnp.transpose(rows_home.reshape(block_x, KY, planes, 2), (1, 2, 3, 0)).reshape(
        KY, planes * 2 * block_x
    )
    real_c, imag_c = inverse_complex(rows_home, cos_y, sin_y, (KY, planes, 2, block_x), 2)
    leaving = jnp.stack([real_c, imag_c], axis=2).reshape(KY, planes * 2 * block_x)
    home = lax.all_to_all(leaving, "pen", split_axis=0, concat_axis=1, tiled=True).reshape(
        block_y, slot_total, 2, block_x
    )
    potential = jnp.einsum(
        "ykx,kz->xyz", home[:, :, 0], plane_weight[:, None] * cos_z, precision=highest
    )
    potential = potential - jnp.einsum(
        "ykx,kz->xyz", home[:, :, 1], plane_weight[:, None] * sin_z, precision=highest
    )
    return (potential, spectral)


def place_tiles(spread, tiles_x, tiles_y):
    shaped = spread.reshape(tiles_x, tiles_y, 4, 2, 4, 2, KZ)
    total = 0.0
    for i in range(4):
        for j in range(4):
            part = jnp.transpose(shaped[:, :, i, :, j], (0, 2, 1, 3, 4)).reshape(
                2 * tiles_x, 2 * tiles_y, KZ
            )
            total = total + jnp.pad(part, ((2 * i, 6 - 2 * i), (2 * j, 6 - 2 * j), (0, 0)))
    return total


def gather_tiles(extended, tiles_x, tiles_y):
    blocks = []
    for i in range(4):
        members = []
        for j in range(4):
            part = extended[2 * i : 2 * i + 2 * tiles_x, 2 * j : 2 * j + 2 * tiles_y]
            part = part.reshape(tiles_x, 2, tiles_y, 2, KZ)
            members.append(jnp.transpose(part, (0, 2, 1, 3, 4)))
        blocks.append(jnp.stack(members, axis=3))
    return jnp.stack(blocks, axis=2).reshape(tiles_x, tiles_y, 64, KZ)


def local(cell_offsets, cell_z, frac, charges, tile_counts):
    block_x = KX // lax.axis_size("grp")
    block_y = KY // lax.axis_size("pen")
    tiles_x = block_x // 2
    tiles_y = block_y // 2
    slots = charges.shape[0] // (tiles_x * tiles_y)
    offsets = cell_offsets.reshape(2, tiles_x, tiles_y, slots)
    zcell = cell_z.reshape(tiles_x, tiles_y, slots)
    fracs = frac.reshape(3, tiles_x, tiles_y, slots)
    charge = charges.reshape(tiles_x, tiles_y, slots)
    counts = tile_counts.reshape(tiles_x, tiles_y)
    weight_x, grade_x, weight_y, grade_y, weight_z, grade_z, live_q = tile_weights(
        offsets, zcell, fracs, charge, counts, KZ
    )
    pair = weight_x[..., :, None, :] * weight_y[..., None, :, :] * live_q[..., None, None, :]
    pair = pair.reshape(tiles_x, tiles_y, 64, slots)
    spread = jnp.einsum("abfs,absz->abfz", pair, weight_z, precision=highest)
    padded = place_tiles(spread, tiles_x, tiles_y)
    rim_y = shifted(padded[: block_x + 5, block_y : block_y + 5], "pen", 1)
    merged = padded[: block_x + 5, :block_y].at[:, :5].add(rim_y)
    rim_x = shifted(merged[block_x : block_x + 5], "grp", 1)
    grid = merged[:block_x].at[:5].add(rim_x)
    potential, spectral = spectrum_pen_first(grid, block_x, block_y)
    upper = shifted(potential[:5], "grp", -1)
    ext_x = jnp.concatenate([potential, upper, jnp.zeros((1, block_y, KZ), jnp.float32)], axis=0)
    beside = shifted(ext_x[:, :5], "pen", -1)
    extended = jnp.concatenate(
        [ext_x, beside, jnp.zeros((block_x + 6, 1, KZ), jnp.float32)], axis=1
    )
    footing = gather_tiles(extended, tiles_x, tiles_y)
    main = jnp.einsum("abfz,absz->abfs", footing, weight_z, precision=highest).reshape(
        tiles_x, tiles_y, 8, 8, slots
    )
    tilt = jnp.einsum("abfz,absz->abfs", footing, grade_z, precision=highest).reshape(
        tiles_x, tiles_y, 8, 8, slots
    )
    force_x = -live_q * jnp.einsum(
        "abxs,abys,abxys->abs", grade_x, weight_y, main, precision=highest
    )
    force_y = -live_q * jnp.einsum(
        "abxs,abys,abxys->abs", weight_x, grade_y, main, precision=highest
    )
    force_z = -live_q * jnp.einsum(
        "abxs,abys,abxys->abs", weight_x, weight_y, tilt, precision=highest
    )
    total = lax.psum(spectral, ("grp", "pen"))
    forces = jnp.stack([force_x, force_y, force_z], axis=0).reshape(3, tiles_x * tiles_y * slots)
    return (forces, total / ATOMS)


def solution(mesh):
    in_specs = (
        P(None, ("grp", "pen")),
        P(("grp", "pen")),
        P(None, ("grp", "pen")),
        P(("grp", "pen")),
        P(("grp", "pen")),
    )
    out_specs = (P(None, ("grp", "pen")), P())
    return jax.shard_map(local, mesh=mesh, in_specs=in_specs, out_specs=out_specs, check_vma=False)
```

profile of v0, /device:TPU:0, one launch (start us, length us, event | category | flops | bytes accessed | tf_op | source)
XLA Modules:
  0.0 1138.8 jit_solution(11327651914012425456)
XLA Ops:
  22.6 140.7 %fusion.15 = f32[32,16,64,256]{3,2,1,0:T(8,128)} fusion(f32[32,16,64]{2,1,0:T(8,128)S(1)} %copy-done.60, s32[32,16,64]{2,1,0:T(8,128)S(1)} %get-tuple-element.184, f32[32,16,64]{2,1,0:T(8,128)S(1)} %copy-done.58, s32[32,16,64]{2,1,0:T(8,128)S(1)} %get-tuple-element.183, f32[32,16,64]{2,1,0:T(8,128)S(1)} %copy-done.54, ...), kind=kOutput, calls=%fused_computation.27 | convolution fusion | flops 6589251584 | bytes 37355520 | tf_op jit(solution)/shard_map/abfs,absz->abfz/dot_general | solution.py:223
  163.2 39.0 %reshape.1907 = f32[32,16,4,2,4,2,256]{6,5,4,3,2,1,0:T(2,128)} reshape(f32[32,16,64,256]{3,2,1,0:T(8,128)} %fusion.15) | data formatting | bytes 67108864 | tf_op jit(solution)/shard_map/reshape | solution.py:184
  202.2 25.3 %slice_bitcast_fusion.15 = (f32[32,2,16,2,256]{4,3,1,2,0:T(2,128)S(1)}, f32[32,2,16,2,256]{4,3,1,2,0:T(2,128)S(1)}, f32[32,2,16,2,256]{4,3,1,2,0:T(2,128)}, f32[...) fusion(f32[32,16,4,2,4,2,256]{6,5,4,3,2,1,0:T(2,128)} %reshape.1907), kind=kLoop, calls=%fused_computation.93 | loop fusion | bytes 67108864 | tf_op jit(solution)/shard_map/transpose | solution.py:188
  233.6 4.0 copy.275
  241.3 4.1 copy.276
  245.3 3.8 reshape.1910
  249.2 4.0 copy.277
  253.1 3.7 reshape.1911
  256.9 4.1 copy.278
  264.7 4.0 copy.279
  272.3 4.0 copy.280
  280.0 4.0 copy.281
  287.6 4.0 copy.282
  291.7 4.0 reshape.1916
  295.7 4.0 copy.283
  303.4 4.1 copy.284
  311.1 4.0 copy.285
  315.1 3.7 reshape.1919
  318.8 4.1 copy.286
  326.6 4.0 copy.287
  330.6 3.7 reshape.1921
  334.3 4.0 copy.288
  338.3 3.8 reshape.1922
  348.2 12.9 %pad_add_fusion = f32[70,38,256]{2,0,1:T(8,128)S(1)} fusion(f32[64,32,256]{2,0,1:T(8,128)} %reshape.1923, f32[64,32,256]{2,0,1:T(8,128)} %reshape.1922, f32[64,32,256]{2,0,1:T(8,128)} %reshape.1921, f32[64,32,256]{2,0,1:T(8,128)} %reshape.1920, f32[64,32,256]{2,0,1:T(8,128)} %reshape.1919, f32[64,32,256]{2,0,1:T(8,128)} %reshape.1918, ...), kind=kLoop, calls=%fused_computation.52 | loop fusion | flops 10214400 | bytes 36278272 | tf_op jit(solution)/shard_map/add | solution.py:191
  365.0 4.7 collective-permute-done
  375.6 5.0 collective-permute-done.1
  389.0 7.5 copy.290
  396.5 4.6 all_to_all.52
  401.6 31.4 %all_to_all.70 = f32[32,8,2176]{2,0,1:T(8,128)} all-to-all(f32[32,8,2176]{2,0,1:T(8,128)S(1)} %copy.291), channel_id=1, replica_groups=mesh['grp'=4,'pen'=8] {'pen'}, dimensions={1} | all-to-all | bytes 4456448 | tf_op jit(solution)/shard_map/all_to_all | solution.py:148
  441.5 5.1 copy.296
  446.6 5.1 copy.297
  451.8 4.0 all-to-all-start.1
  456.4 50.4 %all-to-all-done.1 = f32[64,4,2176]{2,0,1:T(8,128)S(1)} async-done(((f32[64,4,2176]{2,0,1:T(8,128)}), f32[64,4,2176]{2,0,1:T(8,128)S(1)}, u32[]{:S(2)}, u32[]{:S(2)}) %all-to-all-start.1) | async-done | bytes 2228256 | tf_op jit(solution)/shard_map/all_to_all | solution.py:153
  535.2 4.9 all_to_all.60
  540.0 4.5 copy.311
  544.6 54.0 %all_to_all.71 = f32[4,64,2176]{2,1,0:T(8,128)} all-to-all(f32[4,64,2176]{2,1,0:T(8,128)S(1)} %copy.311), channel_id=1, replica_groups=mesh['grp'=4,'pen'=8] {'grp'}, dimensions={0} | all-to-all | bytes 4456448 | tf_op jit(solution)/shard_map/all_to_all | solution.py:165
  598.6 4.7 copy.312
  603.4 7.0 copy.372
  610.4 6.1 copy.313
  616.5 4.6 fusion.36
  624.8 5.1 copy.317
  629.9 4.6 all_to_all.63
  634.5 30.8 %all_to_all.72 = f32[8,32,2176]{2,1,0:T(8,128)S(1)} all-to-all(f32[8,32,2176]{2,1,0:T(8,128)S(1)} %all_to_all.63), channel_id=1, replica_groups=mesh['grp'=4,'pen'=8] {'pen'}, dimensions={0} | all-to-all | bytes 4456448 | tf_op jit(solution)/shard_map/all_to_all | solution.py:171
  666.6 4.1 reshape.1927
  670.7 8.8 fusion.280
  679.5 5.8 copy.378
  685.4 5.3 fusion.141
  690.6 4.5 copy.377
  695.1 4.2 fusion.143
  701.5 55.4 %select_add_fusion.1.clone.4 = f32[32,16,64,256]{3,2,1,0:T(8,128)} fusion(f32[32,16,64]{2,1,0:T(8,128)S(1)} %copy-done.61, s32[32,16,64]{2,1,0:T(8,128)S(1)} %copy-done.43, f32[32,16,64]{2,1,0:T(8,128)S(1)} %copy-done.59, s32[32,16,64]{2,1,0:T(8,128)S(1)} %copy-done.41, f32[32,16,64]{2,1,0:T(8,128)S(1)} %copy-done.55, ...), kind=kLoop, calls=%fused_computation.13.clone.clone.clone.clone.1 | loop fusion | flops 142606336 | bytes 35127296 | tf_op jit(solution)/shard_map/abxs,abys,abxys->abs/dot_general | solution.py:243
  758.3 55.3 %fusion.294 = f32[32,16,64,256]{3,2,1,0:T(8,128)} fusion(f32[32,16,64]{2,1,0:T(8,128)S(1)} %copy-done.53, f32[32,16,64]{2,1,0:T(8,128)S(1)} %copy-done.51, f32[32,16,64]{2,1,0:T(8,128)S(1)} %copy-done.50, f32[32,16,64]{2,1,0:T(8,128)S(1)} %copy-done.52, f32[32,16,64]{2,1,0:T(8,128)S(1)} %copy-done.49, f32[32,16,64]{2,1,0:T(8,128)S(1)} %copy-done.48, ...), kind=kLoop, calls=%fused_computation.2.clone.clone.clone.1 | loop fusion | flops 142606336 | bytes 35127296 | tf_op jit(solution)/shard_map/abfz,absz->abfs/dot_general | solution.py:240
  814.3 38.4 %psum.7 = f32[]{:T(128)} all-reduce(f32[]{:T(128)S(6)} %mul_shard_map.3), channel_id=1, replica_groups=mesh['grp'=4,'pen'=8] {'grp','pen'}, use_global_device_ids=true, to_apply=%region_1.6 | all-reduce | flops 1 | bytes 8 | tf_op jit(solution)/shard_map/psum | solution.py:252
  869.1 6.2 fusion.282
  906.4 3.8 reshape.1941
  916.1 6.8 maximum_bitcast_fusion
  922.9 4.5 maximum_bitcast_fusion.1
  927.5 5.3 maximum_bitcast_fusion.2
  933.8 5.2 maximum_bitcast_fusion.3
  939.1 18.5 %pad_maximum_fusion = f32[32,16,4,2,4,2,256]{6,3,0,5,1,4,2:T(2,128)} fusion(f32[32,16,1,2,4,2,256]{6,3,0,5,1,4,2:T(2,128)} %maximum_bitcast_fusion.3, f32[32,16,1,2,4,2,256]{6,3,0,5,1,4,2:T(2,128)} %maximum_bitcast_fusion.2, f32[32,16,1,2,4,2,256]{6,3,0,5,1,4,2:T(2,128)S(1)} %maximum_bitcast_fusion.1, f32[32,16,1,2,4,2,256]{6,3,0,5,1,4,2:T(2,128)S(1)} %maximum_bitcast_fusion), kind=kLoop, calls=%fused_computation | loop fusion | flops 25165824 | bytes 67108864 | tf_op jit(solution)/shard_map/stack | solution.py:204
  957.5 46.1 %copy.321 = f32[32,16,4,2,4,2,256]{6,5,4,3,2,1,0:T(2,128)} copy(f32[32,16,4,2,4,2,256]{6,3,0,5,1,4,2:T(2,128)} %pad_maximum_fusion) | data formatting | bytes 67108864 | tf_op jit(solution)/shard_map/stack | solution.py:204
  1003.6 39.9 %reshape.1944 = f32[32,16,64,256]{3,2,1,0:T(8,128)} reshape(f32[32,16,4,2,4,2,256]{6,5,4,3,2,1,0:T(2,128)} %copy.321) | data formatting | bytes 67108864 | tf_op jit(solution)/shard_map/reshape | solution.py:204
  1043.6 42.5 %fusion.12 = f32[32,16,64,8]{2,3,1,0:T(8,128)} fusion(f32[32,16,64,8]{2,3,1,0:T(8,128)S(1)} %bitcast.442, f32[32,16,64,256]{3,2,1,0:T(8,128)} %reshape.1944, f32[32,16,64,256]{3,2,1,0:T(8,128)} %fusion.294), kind=kOutput, calls=%fused_computation.21 | convolution fusion | flops 6446383104 | bytes 69206016 | tf_op jit(solution)/shard_map/abfz,absz->abfs/dot_general | solution.py:240
  1086.1 41.7 %fusion.13 = (f32[32,16,64,8]{2,3,1,0:T(8,128)}, f32[32,16,64,8]{2,3,1,0:T(8,128)}) fusion(f32[32,16,64,8]{2,3,1,0:T(8,128)} %get-tuple-element.128, f32[32,16,64,8]{2,3,1,0:T(8,128)S(1)} %bitcast.443, f32[32,16,64,256]{3,2,1,0:T(8,128)} %reshape.1944, f32[32,16,64,256]{3,2,1,0:T(8,128)} %select_add_fusion.1.clone.4), kind=kOutput, calls=%fused_computation.24 | convolution fusion | flops 6450315264 | bytes 71303168 | tf_op jit(solution)/shard_map/abfz,absz->abfs/dot_general | solution.py:237
  1127.9 4.9 multiply_reduce_fusion.2
  (311 shorter events, 185.4 us)
Async XLA Ops:
  10.0 3.7 copy-start.20
  13.3 7.9 copy-start.32
  13.3 7.9 copy-start.34
  13.3 7.8 copy-start.36
  13.3 7.8 copy-start.38
  13.4 7.8 copy-start.40
  13.4 7.8 copy-start.42
  13.5 3.9 copy-start.44
  13.6 3.8 copy-start.90
  13.8 3.6 copy-start.47
  13.8 3.6 copy-start.66
  13.8 3.6 copy-start.67
  13.8 3.6 copy-start.68
  13.8 3.6 copy-start.69
  13.8 3.6 copy-start.70
  13.8 3.6 copy-start.71
  13.9 3.6 copy-start.72
  13.9 3.6 copy-start.73
  13.9 3.6 copy-start.74
  13.9 3.6 copy-start.75
  13.9 3.6 copy-start.76
  13.9 3.6 copy-start.77
  13.9 3.6 copy-start.78
  13.9 3.6 copy-start.79
  13.9 3.6 copy-start.80
  17.6 4.9 copy-start.54
  17.6 4.9 copy-start.56
  17.6 4.9 copy-start.58
  17.6 4.9 copy-start.60
  17.6 4.9 copy-start.62
  17.7 4.9 copy-start.64
  361.1 8.6 collective-permute-start
  371.5 9.1 collective-permute-start.1
  451.8 55.0 %all-to-all-start.1 = ((f32[64,4,2176]{2,0,1:T(8,128)}), f32[64,4,2176]{2,0,1:T(8,128)S(1)}, u32[]{:S(2)}, u32[]{:S(2)}) async-start(f32[64,4,2176]{2,0,1:T(8,128)} %copy.297), calls=%async_computation.1 | async-start | bytes 4456448 | tf_op jit(solution)/shard_map/all_to_all | solution.py:153
  695.1 4.3 copy-start.6
  699.9 57.0 %collective-permute-start.2 = (f32[5,32,256]{2,0,1:T(8,128)S(1)}, f32[5,32,256]{2,0,1:T(8,128)S(1)}, u32[]{:S(2)}, u32[]{:S(2)}) collective-permute-start(f32[5,32,256]{2,0,1:T(8,128)S(1)} %slice.369), channel_id=1, source_target_pairs={{8,0},{16,8},{24,16},{0,24},{9,1},{17,9},{25,17},{1,25},{10,2},{18... | collective-permute-start | bytes 491528 | tf_op jit(solution)/shard_map/ppermute | solution.py:18
  757.0 111.8 %collective-permute-start.3 = (f32[70,5,256]{2,0,1:T(8,128)S(1)}, f32[70,5,256]{2,0,1:T(8,128)S(1)}, u32[]{:S(2)}, u32[]{:S(2)}) collective-permute-start(f32[70,5,256]{2,0,1:T(8,128)S(1)} %pad_maximum_fusion.10), channel_id=1, source_target_pairs={{1,0},{2,1},{3,2},{4,3},{5,4},{6,5},{7,6},{0,7},{9,8},{10,9},{11,1... | collective-permute-start | bytes 1075208 | tf_op jit(solution)/shard_map/ppermute | solution.py:18
  906.4 3.8 copy-start.2
  916.0 6.8 copy-start.10
  916.0 6.8 copy-start.11
  916.1 6.8 copy-start.12
  916.1 6.8 copy-start.14
  922.9 4.5 copy-start.8
  922.9 4.5 copy-start.13
  922.9 4.5 copy-start.15
  922.9 4.5 copy-start.17
  927.4 5.3 copy-start.7
  927.4 5.3 copy-start.16
  927.5 5.6 copy-start.18
  927.5 6.4 copy-start.19
  1003.6 39.9 %copy-start.1 = (f32[32,16,8,64]{3,2,1,0:T(8,128)S(1)}, f32[32,16,8,64]{3,2,1,0:T(8,128)}, u32[]{:S(2)}) copy-start(f32[32,16,8,64]{3,2,1,0:T(8,128)} %copy-done) | copy-start | bytes 3145732
  1086.1 41.7 %copy-start.21 = (s32[32,16,64]{2,1,0:T(8,128)S(1)}, s32[32,16,64]{2,1,0:T(8,128)}, u32[]{:S(2)}) copy-start(s32[32,16,64]{2,1,0:T(8,128)} %copy-done.20) | copy-start | bytes 393220
  1086.1 41.7 %copy-start.23 = (s32[32,16,64]{2,1,0:T(8,128)S(1)}, s32[32,16,64]{2,1,0:T(8,128)}, u32[]{:S(2)}) copy-start(s32[32,16,64]{2,1,0:T(8,128)} %copy-done.22) | copy-start | bytes 393220
  1086.1 41.7 %copy-start.25 = (s32[32,16,64]{2,1,0:T(8,128)S(1)}, s32[32,16,64]{2,1,0:T(8,128)}, u32[]{:S(2)}) copy-start(s32[32,16,64]{2,1,0:T(8,128)} %copy-done.24) | copy-start | bytes 393220
  1086.1 41.7 %copy-start.27 = (s32[32,16,64]{2,1,0:T(8,128)S(1)}, s32[32,16,64]{2,1,0:T(8,128)}, u32[]{:S(2)}) copy-start(s32[32,16,64]{2,1,0:T(8,128)} %copy-done.26) | copy-start | bytes 393220
  1086.1 41.7 %copy-start.29 = (s32[32,16,64]{2,1,0:T(8,128)S(1)}, s32[32,16,64]{2,1,0:T(8,128)}, u32[]{:S(2)}) copy-start(s32[32,16,64]{2,1,0:T(8,128)} %copy-done.28) | copy-start | bytes 393220
  1127.8 4.9 copy-start.4
  1127.8 4.9 copy-start.31
  1127.8 4.9 copy-start.83
  1127.8 4.9 copy-start.84
  1127.9 4.9 copy-start.85
  1127.9 4.9 copy-start.86
  1127.9 4.9 copy-start.87
  1127.9 4.9 copy-start.88
  (36 other events, 86.2 us)
where the time goes:
time: 1150 us; the launch traced here: 1140 us
  local copies, waits for them, and re-layouts  445 us (39%)
  matrix products  265 us (23%)
  other arithmetic  200 us (17%)
  blocking collectives  155 us (13%)
  waiting for transfers between devices  60.1 us (5%)
    dot_general x1, matrix products, local(): spread = jnp.einsum('abfs,absz->abfz', pair, weight_z, precision=highest)  141 us
    transpose x17, local copies, waits for them, and re-layouts, place_tiles(): jnp.transpose(shaped[:, :, i, :, j], (0, 2, 1, 3, 4))  86.3 us
    dot_general x2, other arithmetic, local(): jnp.einsum('abxs,abys,abxys->abs', grade_x, weight_y, main, precision=hig...  60.3 us
    reshape x16, local copies, waits for them, and re-layouts, place_tiles(): jnp.transpose(shaped[:, :, i, :, j], (0, 2, 1, 3, 4))  59.5 us
    dot_general x1, other arithmetic, local(): jnp.einsum('abfz,absz->abfs', footing, grade_z, precision=highest)  55.3 us
    all_to_all x1, blocking collectives, spectrum_pen_first(): lax.all_to_all(returning, 'grp', split_axis=0, concat_axis=1, tiled=True)  54 us
    all_to_all x1, waiting for transfers between devices, spectrum_pen_first(): lax.all_to_all(sectioned, 'grp', split_axis=1, concat_axis=0, tiled=True)  50.4 us
    reshape x16, local copies, waits for them, and re-layouts, gather_tiles(): part = part.reshape(tiles_x, 2, tiles_y, 2, KZ)  50 us
  transfers between devices with their start and end apart: 5, of which 3 were waited for; matrix products, arithmetic and copies ran while one was open for 12% of the time, Pallas kernels for 0%

commit v1 on v0

--- a/solution.py
+++ b/solution.py
@@ -10,6 +10,28 @@
 ATOMS = 1048576
 ewald_split = 0.6
 highest = lax.Precision.HIGHEST
+
+
+def in_blocks(value, dim, size):
+    before, after = (value.shape[:dim], value.shape[dim + 1 :])
+    return jnp.moveaxis(value.reshape(*before, size, -1, *after), dim, 0)
+
+
+def joined_along(tiles, dim):
+    dims = list(tiles.shape[1:])
+    dims[dim] *= tiles.shape[0]
+    return jnp.moveaxis(tiles, 0, dim).reshape(dims)
+
+
+def pairwise_exchange(x, axis, split_dim, concat_dim):
+    size, here = (lax.axis_size(axis), lax.axis_index(axis))
+    blocks = in_blocks(x, split_dim, size)
+    outs = [blocks[here]]
+    for lap in range(1, size):
+        sent = blocks[here ^ lap]
+        outs.append(lax.ppermute(sent, axis, [(i, i ^ lap) for i in range(size)]))
+    blocks = jnp.stack(outs)[here ^ jnp.arange(size)]
+    return joined_along(blocks, concat_dim)
 
 
 def shifted(block, axis, distance):
@@ -162,7 +184,7 @@
     scaled = jnp.stack([kernel * real_x, kernel * imag_x], axis=-1).reshape(KX, lines * planes * 2)
     real_b, imag_b = inverse_complex(scaled, cos_x, sin_x, (KX, lines, planes, 2), 3)
     returning = jnp.stack([real_b, imag_b], axis=-1).reshape(KX, lines * planes * 2)
-    rows_home = lax.all_to_all(returning, "grp", split_axis=0, concat_axis=1, tiled=True)
+    rows_home = pairwise_exchange(returning, "grp", 0, 1)
     rows_home = jnp.transpose(rows_home.reshape(block_x, KY, planes, 2), (1, 2, 3, 0)).reshape(
         KY, planes * 2 * block_x
     )

time: 1150 us -> 1160 us (level)
  blocking collectives: 155 us -> 110 us
  waiting for transfers between devices: 60.1 us -> 92.6 us
  local copies, waits for them, and re-layouts: 445 us -> 465 us
    all_to_all x1 -> x0, blocking collectives: 54 us -> none  [spectrum_pen_first(): lax.all_to_all(returning, 'grp', split_axis=0, concat_axis=1, tiled=True)]
    ppermute x0 -> x3, waiting for transfers between devices: none -> 32.6 us  [pairwise_exchange(): outs.append(lax.ppermute(sent, axis, [(i, i ^ lap) for i in range(size)]))]
    dynamic_slice x0 -> x4, local copies, waits for them, and re-layouts: none -> 19.4 us  [the longest x1 11.5 us: pairwise_exchange(): outs = [blocks[here]]]
    all_to_all x3 -> x0, local copies, waits for them, and re-layouts: 14.1 us -> none  [spectrum_pen_first(): lax.all_to_all(returning, 'grp', split_axis=0, concat_axis=1, tiled=True)]
  transfers between devices with their start and end apart: 5 -> 8, of which waited for: 3 -> 5; matrix products, arithmetic and copies ran while one was open for 12% -> 12% of each run, Pallas kernels for 0% -> 0%
where the time goes in v1:
time: 1160 us; the launch traced here: 1150 us
  local copies, waits for them, and re-layouts  465 us (40%)
  matrix products  265 us (23%)
  other arithmetic  202 us (17%)
  blocking collectives  110 us (9%)
  waiting for transfers between devices  92.6 us (8%)
  starting transfers between devices  13.1 us (1%)
    dot_general x1, matrix products, local(): spread = jnp.einsum('abfs,absz->abfz', pair, weight_z, precision=highest)  141 us
    transpose x17, local copies, waits for them, and re-layouts, place_tiles(): jnp.transpose(shaped[:, :, i, :, j], (0, 2, 1, 3, 4))  86.4 us
    dot_general x2, other arithmetic, local(): jnp.einsum('abxs,abys,abxys->abs', grade_x, weight_y, main, precision=hig...  60.2 us
    reshape x16, local copies, waits for them, and re-layouts, place_tiles(): jnp.transpose(shaped[:, :, i, :, j], (0, 2, 1, 3, 4))  59.6 us
    dot_general x1, other arithmetic, local(): jnp.einsum('abfz,absz->abfs', footing, grade_z, precision=highest)  55.3 us
    all_to_all x1, waiting for transfers between devices, spectrum_pen_first(): lax.all_to_all(sectioned, 'grp', split_axis=1, concat_axis=0, tiled=True)  50.4 us
    reshape x16, local copies, waits for them, and re-layouts, gather_tiles(): part = part.reshape(tiles_x, 2, tiles_y, 2, KZ)  50.1 us
    psum x1, blocking collectives, local(): total = lax.psum(spectral, ('grp', 'pen'))  48.1 us
  transfers between devices with their start and end apart: 8, of which 5 were waited for; matrix products, arithmetic and copies ran while one was open for 12% of the time, Pallas kernels for 0%

profile of v1, /device:TPU:0, one launch (start us, length us, event | category | flops | bytes accessed | tf_op | source)
XLA Modules:
  0.0 1151.9 jit_solution(1173826163659423191)
XLA Ops:
  22.6 140.6 %fusion.15 = f32[32,16,64,256]{3,2,1,0:T(8,128)} fusion(f32[32,16,64]{2,1,0:T(8,128)S(1)} %copy-done.60, s32[32,16,64]{2,1,0:T(8,128)S(1)} %get-tuple-element.188, f32[32,16,64]{2,1,0:T(8,128)S(1)} %copy-done.58, s32[32,16,64]{2,1,0:T(8,128)S(1)} %get-tuple-element.187, f32[32,16,64]{2,1,0:T(8,128)S(1)} %copy-done.54, ...), kind=kOutput, calls=%fused_computation.28 | convolution fusion | flops 6589251584 | bytes 37355520 | tf_op jit(solution)/shard_map/abfs,absz->abfz/dot_general | solution.py:245
  163.3 39.0 %reshape.1914 = f32[32,16,4,2,4,2,256]{6,5,4,3,2,1,0:T(2,128)} reshape(f32[32,16,64,256]{3,2,1,0:T(8,128)} %fusion.15) | data formatting | bytes 67108864 | tf_op jit(solution)/shard_map/reshape | solution.py:206
  202.2 25.3 %slice_bitcast_fusion.15 = (f32[32,2,16,2,256]{4,3,1,2,0:T(2,128)S(1)}, f32[32,2,16,2,256]{4,3,1,2,0:T(2,128)S(1)}, f32[32,2,16,2,256]{4,3,1,2,0:T(2,128)}, f32[...) fusion(f32[32,16,4,2,4,2,256]{6,5,4,3,2,1,0:T(2,128)} %reshape.1914), kind=kLoop, calls=%fused_computation.95 | loop fusion | bytes 67108864 | tf_op jit(solution)/shard_map/transpose | solution.py:210
  233.7 4.0 copy.288
  241.3 4.1 copy.289
  245.4 3.8 reshape.1917
  249.2 4.0 copy.290
  253.2 3.7 reshape.1918
  257.0 4.1 copy.291
  264.7 4.0 copy.292
  272.4 4.0 copy.293
  280.1 4.0 copy.294
  287.8 4.0 copy.295
  291.8 4.1 reshape.1923
  295.9 4.0 copy.296
  303.6 4.1 copy.297
  311.3 4.0 copy.298
  315.3 3.7 reshape.1926
  319.0 4.1 copy.299
  326.8 4.0 copy.300
  334.5 4.0 copy.301
  338.4 3.8 reshape.1929
  348.3 12.9 %pad_add_fusion = f32[70,38,256]{2,0,1:T(8,128)S(1)} fusion(f32[64,32,256]{2,0,1:T(8,128)} %reshape.1930, f32[64,32,256]{2,0,1:T(8,128)} %reshape.1929, f32[64,32,256]{2,0,1:T(8,128)} %reshape.1928, f32[64,32,256]{2,0,1:T(8,128)} %reshape.1927, f32[64,32,256]{2,0,1:T(8,128)} %reshape.1926, f32[64,32,256]{2,0,1:T(8,128)} %reshape.1925, ...), kind=kLoop, calls=%fused_computation.53 | loop fusion | flops 10214400 | bytes 36278272 | tf_op jit(solution)/shard_map/add | solution.py:213
  365.2 4.7 collective-permute-done
  375.9 5.0 collective-permute-done.1
  389.3 7.5 copy.303
  396.8 4.6 all_to_all.40
  401.9 31.4 %all_to_all.54 = f32[32,8,2176]{2,0,1:T(8,128)} all-to-all(f32[32,8,2176]{2,0,1:T(8,128)S(1)} %copy.304), channel_id=1, replica_groups=mesh['grp'=4,'pen'=8] {'pen'}, dimensions={1} | all-to-all | bytes 4456448 | tf_op jit(solution)/shard_map/all_to_all | solution.py:170
  441.8 5.0 copy.309
  446.9 5.1 copy.310
  451.9 4.0 all-to-all-start.1
  456.6 50.4 %all-to-all-done.1 = f32[64,4,2176]{2,0,1:T(8,128)S(1)} async-done(((f32[64,4,2176]{2,0,1:T(8,128)}), f32[64,4,2176]{2,0,1:T(8,128)S(1)}, u32[]{:S(2)}, u32[]{:S(2)}) %all-to-all-start.1) | async-done | bytes 2228256 | tf_op jit(solution)/shard_map/all_to_all | solution.py:175
  535.3 4.8 reshape_reshape.6
  540.2 11.5 constant_dynamic-slice_fusion
  565.3 12.1 %collective-permute-done.2 = f32[64,2176]{1,0:T(8,128)} collective-permute-done((f32[64,2176]{1,0:T(8,128)}, f32[64,2176]{1,0:T(8,128)}, u32[]{:S(2)}, u32[]{:S(2)}) %collective-permute-start.2) | collective-permute-done | bytes 557088 | tf_op jit(solution)/shard_map/ppermute | solution.py:32
  577.4 20.5 %collective-permute-done.3 = f32[64,2176]{1,0:T(8,128)S(1)} collective-permute-done((f32[64,2176]{1,0:T(8,128)}, f32[64,2176]{1,0:T(8,128)S(1)}, u32[]{:S(2)}, u32[]{:S(2)}) %collective-permute-start.3) | collective-permute-done | bytes 557088 | tf_op jit(solution)/shard_map/ppermute | solution.py:32
  602.1 4.7 copy.328
  606.8 7.0 copy.388
  613.9 6.1 copy.329
  620.0 4.6 fusion.36
  628.2 5.0 copy.333
  633.3 5.0 all_to_all.48
  638.3 30.4 %all_to_all.55 = f32[8,32,2176]{2,1,0:T(8,128)S(1)} all-to-all(f32[8,32,2176]{2,1,0:T(8,128)S(1)} %all_to_all.48), channel_id=1, replica_groups=mesh['grp'=4,'pen'=8] {'pen'}, dimensions={0} | all-to-all | bytes 4456448 | tf_op jit(solution)/shard_map/all_to_all | solution.py:193
  670.0 4.1 reshape.1933
  674.1 8.8 fusion.281
  682.9 5.8 copy.395
  688.7 5.3 fusion.141
  694.0 4.4 copy.394
  698.4 4.2 fusion.143
  704.8 55.4 %select_add_fusion.1.clone.4 = f32[32,16,64,256]{3,2,1,0:T(8,128)} fusion(f32[32,16,64]{2,1,0:T(8,128)S(1)} %copy-done.61, s32[32,16,64]{2,1,0:T(8,128)S(1)} %copy-done.43, f32[32,16,64]{2,1,0:T(8,128)S(1)} %copy-done.59, s32[32,16,64]{2,1,0:T(8,128)S(1)} %copy-done.41, f32[32,16,64]{2,1,0:T(8,128)S(1)} %copy-done.55, ...), kind=kLoop, calls=%fused_computation.14.clone.clone.clone.clone.1 | loop fusion | flops 142606336 | bytes 35127296 | tf_op jit(solution)/shard_map/abxs,abys,abxys->abs/dot_general | solution.py:265
  761.6 55.3 %fusion.295 = f32[32,16,64,256]{3,2,1,0:T(8,128)} fusion(f32[32,16,64]{2,1,0:T(8,128)S(1)} %copy-done.53, f32[32,16,64]{2,1,0:T(8,128)S(1)} %copy-done.51, f32[32,16,64]{2,1,0:T(8,128)S(1)} %copy-done.50, f32[32,16,64]{2,1,0:T(8,128)S(1)} %copy-done.52, f32[32,16,64]{2,1,0:T(8,128)S(1)} %copy-done.49, f32[32,16,64]{2,1,0:T(8,128)S(1)} %copy-done.48, ...), kind=kLoop, calls=%fused_computation.3.clone.clone.clone.1 | loop fusion | flops 142606336 | bytes 35127296 | tf_op jit(solution)/shard_map/abfz,absz->abfs/dot_general | solution.py:262
  817.6 48.1 %psum.7 = f32[]{:T(128)} all-reduce(f32[]{:T(128)S(6)} %mul_shard_map.3), channel_id=1, replica_groups=mesh['grp'=4,'pen'=8] {'grp','pen'}, use_global_device_ids=true, to_apply=%region_1.6 | all-reduce | flops 1 | bytes 8 | tf_op jit(solution)/shard_map/psum | solution.py:274
  882.1 6.2 fusion.283
  919.4 3.8 reshape.1947
  929.1 6.8 maximum_bitcast_fusion
  936.0 4.5 maximum_bitcast_fusion.1
  940.6 5.3 maximum_bitcast_fusion.2
  946.9 5.2 maximum_bitcast_fusion.3
  952.1 18.5 %pad_maximum_fusion = f32[32,16,4,2,4,2,256]{6,3,0,5,1,4,2:T(2,128)} fusion(f32[32,16,1,2,4,2,256]{6,3,0,5,1,4,2:T(2,128)} %maximum_bitcast_fusion.3, f32[32,16,1,2,4,2,256]{6,3,0,5,1,4,2:T(2,128)} %maximum_bitcast_fusion.2, f32[32,16,1,2,4,2,256]{6,3,0,5,1,4,2:T(2,128)S(1)} %maximum_bitcast_fusion.1, f32[32,16,1,2,4,2,256]{6,3,0,5,1,4,2:T(2,128)S(1)} %maximum_bitcast_fusion), kind=kLoop, calls=%fused_computation.1 | loop fusion | flops 25165824 | bytes 67108864 | tf_op jit(solution)/shard_map/stack | solution.py:226
  970.6 46.1 %copy.337 = f32[32,16,4,2,4,2,256]{6,5,4,3,2,1,0:T(2,128)} copy(f32[32,16,4,2,4,2,256]{6,3,0,5,1,4,2:T(2,128)} %pad_maximum_fusion) | data formatting | bytes 67108864 | tf_op jit(solution)/shard_map/stack | solution.py:226
  1016.7 39.9 %reshape.1950 = f32[32,16,64,256]{3,2,1,0:T(8,128)} reshape(f32[32,16,4,2,4,2,256]{6,5,4,3,2,1,0:T(2,128)} %copy.337) | data formatting | bytes 67108864 | tf_op jit(solution)/shard_map/reshape | solution.py:226
  1056.7 42.5 %fusion.12 = f32[32,16,64,8]{2,3,1,0:T(8,128)} fusion(f32[32,16,64,8]{2,3,1,0:T(8,128)S(1)} %bitcast.450, f32[32,16,64,256]{3,2,1,0:T(8,128)} %reshape.1950, f32[32,16,64,256]{3,2,1,0:T(8,128)} %fusion.295), kind=kOutput, calls=%fused_computation.22 | convolution fusion | flops 6446383104 | bytes 69206016 | tf_op jit(solution)/shard_map/abfz,absz->abfs/dot_general | solution.py:262
  1099.2 41.7 %fusion.13 = (f32[32,16,64,8]{2,3,1,0:T(8,128)}, f32[32,16,64,8]{2,3,1,0:T(8,128)}) fusion(f32[32,16,64,8]{2,3,1,0:T(8,128)} %get-tuple-element.132, f32[32,16,64,8]{2,3,1,0:T(8,128)S(1)} %bitcast.451, f32[32,16,64,256]{3,2,1,0:T(8,128)} %reshape.1950, f32[32,16,64,256]{3,2,1,0:T(8,128)} %select_add_fusion.1.clone.4), kind=kOutput, calls=%fused_computation.25 | convolution fusion | flops 6450315264 | bytes 71303168 | tf_op jit(solution)/shard_map/abfz,absz->abfs/dot_general | solution.py:259
  1141.0 4.9 multiply_reduce_fusion.2
  (326 shorter events, 207.2 us)
Async XLA Ops:
  10.1 3.7 copy-start.20
  13.4 7.8 copy-start.32
  13.4 7.8 copy-start.34
  13.4 7.8 copy-start.36
  13.4 7.8 copy-start.38
  13.4 7.8 copy-start.40
  13.4 7.8 copy-start.42
  13.6 3.9 copy-start.44
  13.6 3.8 copy-start.91
  13.8 3.6 copy-start.47
  13.9 3.6 copy-start.66
  13.9 3.6 copy-start.67
  13.9 3.6 copy-start.68
  13.9 3.6 copy-start.69
  13.9 3.6 copy-start.70
  13.9 3.6 copy-start.71
  13.9 3.6 copy-start.72
  13.9 3.6 copy-start.73
  13.9 3.6 copy-start.74
  13.9 3.6 copy-start.75
  14.0 3.6 copy-start.76
  14.0 3.6 copy-start.77
  17.7 4.9 copy-start.54
  17.7 4.9 copy-start.56
  17.7 4.9 copy-start.58
  17.7 4.9 copy-start.60
  17.7 4.9 copy-start.62
  17.7 4.9 copy-start.64
  361.3 8.6 collective-permute-start
  371.6 9.2 collective-permute-start.1
  451.9 55.0 %all-to-all-start.1 = ((f32[64,4,2176]{2,0,1:T(8,128)}), f32[64,4,2176]{2,0,1:T(8,128)S(1)}, u32[]{:S(2)}, u32[]{:S(2)}) async-start(f32[64,4,2176]{2,0,1:T(8,128)} %copy.310), calls=%async_computation.1 | async-start | bytes 4456448 | tf_op jit(solution)/shard_map/all_to_all | solution.py:175
  555.2 22.2 %collective-permute-start.2 = (f32[64,2176]{1,0:T(8,128)}, f32[64,2176]{1,0:T(8,128)}, u32[]{:S(2)}, u32[]{:S(2)}) collective-permute-start(f32[64,2176]{1,0:T(8,128)} %bitcast.482), channel_id=1, source_target_pairs={{0,8},{8,0},{16,24},{24,16},{1,9},{9,1},{17,25},{25,17},{2,10},{10... | collective-permute-start | bytes 1671176 | tf_op jit(solution)/shard_map/ppermute | solution.py:32
  557.4 40.5 %collective-permute-start.3 = (f32[64,2176]{1,0:T(8,128)}, f32[64,2176]{1,0:T(8,128)S(1)}, u32[]{:S(2)}, u32[]{:S(2)}) collective-permute-start(f32[64,2176]{1,0:T(8,128)} %bitcast.483), channel_id=1, source_target_pairs={{0,16},{8,24},{16,0},{24,8},{1,17},{9,25},{17,1},{25,9},{2,18},{10... | collective-permute-start | bytes 1671176 | tf_op jit(solution)/shard_map/ppermute | solution.py:32
  561.6 36.3 %collective-permute-start.4 = (f32[64,2176]{1,0:T(8,128)}, f32[64,2176]{1,0:T(8,128)S(1)}, u32[]{:S(2)}, u32[]{:S(2)}) collective-permute-start(f32[64,2176]{1,0:T(8,128)} %bitcast.87), channel_id=1, source_target_pairs={{0,24},{8,16},{16,8},{24,0},{1,25},{9,17},{17,9},{25,1},{2,26},{10... | collective-permute-start | bytes 1671176 | tf_op jit(solution)/shard_map/ppermute | solution.py:32
  698.4 4.3 copy-start.6
  703.2 57.1 %collective-permute-start.5 = (f32[5,32,256]{2,0,1:T(8,128)S(1)}, f32[5,32,256]{2,0,1:T(8,128)S(1)}, u32[]{:S(2)}, u32[]{:S(2)}) collective-permute-start(f32[5,32,256]{2,0,1:T(8,128)S(1)} %slice.371), channel_id=1, source_target_pairs={{8,0},{16,8},{24,16},{0,24},{9,1},{17,9},{25,17},{1,25},{10,2},{18... | collective-permute-start | bytes 491528 | tf_op jit(solution)/shard_map/ppermute | solution.py:40
  760.3 121.5 %collective-permute-start.6 = (f32[70,5,256]{2,0,1:T(8,128)S(1)}, f32[70,5,256]{2,0,1:T(8,128)S(1)}, u32[]{:S(2)}, u32[]{:S(2)}) collective-permute-start(f32[70,5,256]{2,0,1:T(8,128)S(1)} %pad_maximum_fusion.11), channel_id=1, source_target_pairs={{1,0},{2,1},{3,2},{4,3},{5,4},{6,5},{7,6},{0,7},{9,8},{10,9},{11,1... | collective-permute-start | bytes 1075208 | tf_op jit(solution)/shard_map/ppermute | solution.py:40
  919.4 3.8 copy-start.2
  929.1 6.8 copy-start.10
  929.1 6.8 copy-start.11
  929.1 6.8 copy-start.12
  929.1 6.8 copy-start.14
  936.0 4.5 copy-start.8
  936.0 4.5 copy-start.13
  936.0 4.5 copy-start.15
  936.0 4.5 copy-start.17
  940.5 5.3 copy-start.7
  940.5 5.3 copy-start.16
  940.5 5.6 copy-start.18
  940.5 6.4 copy-start.19
  1016.7 39.9 %copy-start.1 = (f32[32,16,8,64]{3,2,1,0:T(8,128)S(1)}, f32[32,16,8,64]{3,2,1,0:T(8,128)}, u32[]{:S(2)}) copy-start(f32[32,16,8,64]{3,2,1,0:T(8,128)} %copy-done) | copy-start | bytes 3145732
  1099.2 41.7 %copy-start.21 = (s32[32,16,64]{2,1,0:T(8,128)S(1)}, s32[32,16,64]{2,1,0:T(8,128)}, u32[]{:S(2)}) copy-start(s32[32,16,64]{2,1,0:T(8,128)} %copy-done.20) | copy-start | bytes 393220
  1099.2 41.7 %copy-start.23 = (s32[32,16,64]{2,1,0:T(8,128)S(1)}, s32[32,16,64]{2,1,0:T(8,128)}, u32[]{:S(2)}) copy-start(s32[32,16,64]{2,1,0:T(8,128)} %copy-done.22) | copy-start | bytes 393220
  1099.2 41.7 %copy-start.25 = (s32[32,16,64]{2,1,0:T(8,128)S(1)}, s32[32,16,64]{2,1,0:T(8,128)}, u32[]{:S(2)}) copy-start(s32[32,16,64]{2,1,0:T(8,128)} %copy-done.24) | copy-start | bytes 393220
  1099.2 41.7 %copy-start.27 = (s32[32,16,64]{2,1,0:T(8,128)S(1)}, s32[32,16,64]{2,1,0:T(8,128)}, u32[]{:S(2)}) copy-start(s32[32,16,64]{2,1,0:T(8,128)} %copy-done.26) | copy-start | bytes 393220
  1099.2 41.7 %copy-start.29 = (s32[32,16,64]{2,1,0:T(8,128)S(1)}, s32[32,16,64]{2,1,0:T(8,128)}, u32[]{:S(2)}) copy-start(s32[32,16,64]{2,1,0:T(8,128)} %copy-done.28) | copy-start | bytes 393220
  1140.9 4.9 copy-start.4
  1140.9 4.9 copy-start.31
  1140.9 4.9 copy-start.83
  1141.0 4.9 copy-start.84
  1141.0 4.9 copy-start.85
  1141.0 4.9 copy-start.86
  1141.0 4.9 copy-start.87
  1141.0 4.9 copy-start.88
  (40 other events, 98.3 us)
